TPU v7x, 512 devices: a whole 4x8x8 slice. The times are simulated.
512 devices in a mesh: wl: 16 (over y, core), sec: 32 (over x, z).
Axes of the slice: x: 4, y: 8, z: 8, core: 2. Of those that a mesh axis runs over, the one named last changes fastest.
Arguments:
- sections: float32 [128, 32, 2, 2, 128, 128], P('sec', None, None, None, 'wl'), as said below
- launch_mode: int32 [32], P('wl'), may hold values from 0 to 127
Outputs:
- forward_field: float32 [128, 32, 2, 128], P('sec', 'wl')
- backward_field: float32 [128, 32, 2, 128], P('sec', 'wl')
Inputs may be any that keep to these rules, and one draw needn't show every extreme that they name: `sections`: every entry is finite; each matrix is a unit-modulus diagonal plus a full coupling, scaled so that it keeps a field's power on average.
All inputs are finite; a program needn't handle non-finite values.
Results may differ from a plain program's by a relative error of at most 0.0003.
Values sent between devices are 32-bit elements; how exact they have to be, the bound alone decides.
No kernel may reach another device: no remote copies, remote signals or barrier semaphores. Data moves between devices by JAX's collectives and lax.ppermute only.
A program may use at most 64 MiB of HBM per device.

v0:
```python
import math
import jax
import jax.numpy as jnp
from jax import lax
from jax.sharding import PartitionSpec as P


def entering(part, axis, combine, identity, reverse):
    count = lax.axis_size(axis)
    place = lax.axis_index(axis)
    ahead = count - 1 - place if reverse else place
    gathered = lax.all_gather(part, axis)
    state = jnp.zeros_like(part) + jnp.asarray(identity, part.dtype)

    def one(turn, state):
        source = count - 1 - turn if reverse else turn
        return combine(state, lax.dynamic_index_in_dim(gathered, source, 0, False))

    return lax.fori_loop(0, ahead, one, state)


def matrix_product(outer_mat, inner_mat):
    return jnp.matmul(outer_mat, inner_mat, precision=lax.Precision.HIGHEST)


def complex_product(outer_mat, inner_mat):
    real_part = matrix_product(outer_mat[..., 0, :, :], inner_mat[..., 0, :, :]) - matrix_product(
        outer_mat[..., 1, :, :], inner_mat[..., 1, :, :]
    )
    imag_part = matrix_product(outer_mat[..., 0, :, :], inner_mat[..., 1, :, :]) + matrix_product(
        outer_mat[..., 1, :, :], inner_mat[..., 0, :, :]
    )
    return jnp.stack([real_part, imag_part], axis=-3)


def complex_apply(matrix, vector):
    real_part = jnp.einsum(
        "...ij,...j->...i", matrix[..., 0, :, :], vector[..., 0, :], precision=lax.Precision.HIGHEST
    ) - jnp.einsum(
        "...ij,...j->...i", matrix[..., 1, :, :], vector[..., 1, :], precision=lax.Precision.HIGHEST
    )
    imag_part = jnp.einsum(
        "...ij,...j->...i", matrix[..., 0, :, :], vector[..., 1, :], precision=lax.Precision.HIGHEST
    ) + jnp.einsum(
        "...ij,...j->...i", matrix[..., 1, :, :], vector[..., 0, :], precision=lax.Precision.HIGHEST
    )
    return jnp.stack([real_part, imag_part], axis=-2)


def combine(earlier, latter):
    return complex_product(latter, earlier)


def shards(sections, launch_mode):
    regrouped = lax.all_to_all(sections, "wl", split_axis=1, concat_axis=4, tiled=True)
    forward_mats = regrouped[:, :, 0]
    backward_mats = regrouped[:, :, 1]
    modes = forward_mats.shape[-1]
    onehot = (jnp.arange(modes)[None, :] == launch_mode[:, None]).astype(jnp.float32) * math.sqrt(
        modes
    )
    launch_field = jnp.stack([onehot, jnp.zeros_like(onehot)], axis=1)

    def extend(running, matrix):
        nxt_mat = complex_product(matrix, running)
        return (nxt_mat, nxt_mat)

    last_forward, later_prefix = lax.scan(extend, forward_mats[0], forward_mats[1:])
    prefixes = jnp.concatenate([forward_mats[:1], later_prefix], axis=0)

    def shrink(running, matrix):
        return (complex_product(matrix, running), running)

    suffix_head, suffix_middle = lax.scan(
        shrink, backward_mats[-1], backward_mats[1:-1], reverse=True
    )
    suffixes = jnp.concatenate([suffix_head[None], suffix_middle], axis=0)
    backward_total = complex_product(backward_mats[0], suffix_head)
    unit_matrix = jnp.eye(modes, dtype=jnp.float32)
    identity_mats = jnp.broadcast_to(
        jnp.stack([unit_matrix, jnp.zeros_like(unit_matrix)], axis=0), last_forward.shape
    )
    forward_before = entering(last_forward, "sec", combine, identity_mats, False)
    backward_after = entering(backward_total, "sec", combine, identity_mats, True)
    entry_field = complex_apply(forward_before, launch_field)
    exit_field = complex_apply(backward_after, launch_field)
    forward_field = complex_apply(prefixes, entry_field)
    backward_field = jnp.concatenate(
        [complex_apply(suffixes, exit_field), exit_field[None]], axis=0
    )
    return (forward_field, backward_field)


def solution(mesh):
    return jax.shard_map(
        shards,
        mesh=mesh,
        in_specs=(P("sec", None, None, None, "wl", None), P("wl")),
        out_specs=(P("sec", "wl", None, None), P("sec", "wl", None, None)),
        check_vma=False,
    )
```

profile of v0, /device:TPU:454, one launch (start us, length us, event | category | flops | bytes accessed | tf_op | source)
XLA Modules:
  0.0 357.5 jit_solution(17075956038594746019)
XLA Ops:
  7.2 3.2 copy.14
  10.3 7.2 %all-to-all-start = ((f32[4,32,2,2,8,128]{5,4,3,2,0,1:T(8,128)}), f32[4,32,2,2,8,128]{5,4,3,2,0,1:T(8,128)S(1)}, u32[]{:S(2)}, u32[]{:S(2)}) async-start(f32[4,32,2,2,8,128]{5,4,3,2,0,1:T(8,128)} %copy.14), calls=%async_computation | async-start | bytes 4194304 | tf_op jit(solution)/shard_map/all_to_all | solution.py:55
  17.6 49.2 %all-to-all-done = f32[4,32,2,2,8,128]{5,4,3,2,0,1:T(8,128)S(1)} async-done(((f32[4,32,2,2,8,128]{5,4,3,2,0,1:T(8,128)}), f32[4,32,2,2,8,128]{5,4,3,2,0,1:T(8,128)S(1)}, u32[]{:S(2)}, u32[]{:S(2)}) %all-to-all-start) | async-done | bytes 2097184 | tf_op jit(solution)/shard_map/all_to_all | solution.py:55
  66.8 1.3 copy-done
  68.1 1.8 copy.75
  70.0 0.8 slice_bitcast_fusion.27
  70.8 0.8 broadcast_in_dim.33
  71.6 3.9 %while.52 = (s32[]{:T(128)}, f32[2,2,128,128]{3,2,0,1:T(8,128)S(1)}, f32[2,2,2,128,128]{4,3,1,2,0:T(8,128)}, f32[2,2,2,128,128]{4,3,1,2,0:T(8,128)S(1)}, s32[]{:T(128)}) while((s32[]{:T(128)}, f32[2,2,128,128]{3,2,0,1:T(8,128)S(1)}, f32[2,2,2,128,128]{4,3,1,2,0:T(8,128)}, f32[2,2,2,128,128]{4,3,1,2,0:T(8,128)S(1)}, s32[]{:T(128)}) %tuple.105), condition=%wide.region_5.6_spmd, body=%wide.region_4.5_spmd.sunk | while | flops 201457664 | bytes 7602313 | solution.py:74
  72.8 0.8 copy-done.2
  74.8 0.8 copy-done.2
  75.7 0.4 fusion.89
  76.1 0.4 fusion.88
  76.5 0.4 fusion.48
  76.9 0.4 fusion.49
  77.3 0.7 pad_maximum_fusion.6
  78.2 5.6 %while.50 = (s32[]{:T(128)}, f32[2,2,128,128]{3,2,0,1:T(8,128)S(1)}, f32[3,2,2,128,128]{4,3,1,2,0:T(8,128)}, f32[3,2,2,128,128]{4,3,1,2,0:T(8,128)S(1)}, s32[]{:T(128)}) while((s32[]{:T(128)}, f32[2,2,128,128]{3,2,0,1:T(8,128)S(1)}, f32[3,2,2,128,128]{4,3,1,2,0:T(8,128)}, f32[3,2,2,128,128]{4,3,1,2,0:T(8,128)S(1)}, s32[]{:T(128)}) %tuple.99), condition=%wide.region_1.2_spmd, body=%wide.region_0.1_spmd.sunk | while | flops 201457664 | bytes 3145805 | solution.py:68
  79.3 0.7 bitcast_dynamic-update-slice_fusion.4
  81.2 0.7 bitcast_dynamic-update-slice_fusion.4
  83.0 0.7 bitcast_dynamic-update-slice_fusion.4
  83.8 0.7 copy.16
  84.8 1.2 fusion.51
  86.0 88.7 %all-gather.7.cloned.1.call-done = f32[64,2,128,128]{2,3,0,1:T(8,128)} async-done(((f32[2,2,128,128]{2,3,0,1:T(8,128)}), f32[64,2,128,128]{2,3,0,1:T(8,128)}) %all-gather.7.cloned.1.call-update) | async-done | bytes 8388624 | tf_op jit(solution)/shard_map/all_gather | solution.py:12
  176.0 102.6 %all-gather.5.cloned.1.call-done = f32[64,2,128,128]{3,2,1,0:T(8,128)} async-done(((f32[2,2,128,128]{3,2,1,0:T(8,128)}), f32[64,2,128,128]{3,2,1,0:T(8,128)}) %all-gather.5.cloned.1.call-update) | async-done | bytes 8388624 | tf_op jit(solution)/shard_map/all_gather | solution.py:12
  278.6 65.7 %while.51 = (s32[]{:T(128)}, f32[2,2,128,128]{3,2,0,1:T(8,128)S(1)}, s32[]{:T(128)}, f32[32,2,2,128,128]{4,3,2,1,0:T(8,128)}, s32[]{:T(128)}, /*index=5*/s32[]{:T(128)}, s32[]{:T(128)}) while((s32[]{:T(128)}, f32[2,2,128,128]{3,2,0,1:T(8,128)S(1)}, s32[]{:T(128)}, f32[32,2,2,128,128]{4,3,2,1,0:T(8,128)}, s32[]{:T(128)}, /*index=5*/s32[]{:T(128)}, ...), condition=%wide.region_3.4_spmd, body=%wide.region_2.3_spmd.sunk | while | flops 201457664 | bytes 2883707 | solution.py:19
  278.7 1.0 copy_bitcast_fusion.3
  280.8 1.0 copy_bitcast_fusion.3
  282.9 1.0 copy_bitcast_fusion.3
  285.0 1.0 copy_bitcast_fusion.3
  287.2 1.0 copy_bitcast_fusion.3
  289.3 1.0 copy_bitcast_fusion.3
  291.4 1.0 copy_bitcast_fusion.3
  293.5 1.0 copy_bitcast_fusion.3
  295.6 1.0 copy_bitcast_fusion.3
  297.8 1.0 copy_bitcast_fusion.3
  299.9 1.0 copy_bitcast_fusion.3
  302.0 1.0 copy_bitcast_fusion.3
  304.1 1.0 copy_bitcast_fusion.3
  306.2 1.0 copy_bitcast_fusion.3
  308.4 1.0 copy_bitcast_fusion.3
  310.5 1.0 copy_bitcast_fusion.3
  312.6 1.0 copy_bitcast_fusion.3
  314.7 1.0 copy_bitcast_fusion.3
  316.8 1.0 copy_bitcast_fusion.3
  319.0 1.0 copy_bitcast_fusion.3
  321.1 1.0 copy_bitcast_fusion.3
  323.2 1.0 copy_bitcast_fusion.3
  325.3 1.0 copy_bitcast_fusion.3
  327.4 1.0 copy_bitcast_fusion.3
  329.6 1.0 copy_bitcast_fusion.3
  331.7 1.0 copy_bitcast_fusion.3
  333.8 1.0 copy_bitcast_fusion.3
  335.9 1.0 copy_bitcast_fusion.3
  338.0 1.0 copy_bitcast_fusion.3
  340.2 1.0 copy_bitcast_fusion.3
  342.3 1.0 copy_bitcast_fusion.3
  345.7 0.5 fusion.53
  346.2 0.5 fusion.55
  346.8 0.5 fusion.57
  347.3 0.5 fusion.59
  347.8 0.5 fusion.68
  348.4 0.5 fusion.70
  348.9 0.5 fusion.64
  349.4 0.5 fusion.66
  350.0 0.6 pad_maximum_fusion.7
  (230 shorter events, 42.5 us)
Async XLA Ops:
  10.3 56.4 %all-to-all-start = ((f32[4,32,2,2,8,128]{5,4,3,2,0,1:T(8,128)}), f32[4,32,2,2,8,128]{5,4,3,2,0,1:T(8,128)S(1)}, u32[]{:S(2)}, u32[]{:S(2)}) async-start(f32[4,32,2,2,8,128]{5,4,3,2,0,1:T(8,128)} %copy.14), calls=%async_computation | async-start | bytes 4194304 | tf_op jit(solution)/shard_map/all_to_all | solution.py:55
  17.5 157.1 %all-gather.7.cloned.1.call-start = ((), (), s32[]{:S(2)}) async-start(), calls=%async_computation.2 | async-start | bytes 8650752 | tf_op jit(solution)/shard_map/all_gather | solution.py:12
  66.8 1.3 copy-start
  71.6 1.1 copy-start.1
  72.8 0.8 copy-start.2
  73.6 1.1 copy-start.1
  74.8 0.8 copy-start.2
  78.0 200.6 %all-gather.5.cloned.1.call-start = ((), (), s32[]{:S(2)}) async-start(), calls=%async_computation.1 | async-start | bytes 8650752 | tf_op jit(solution)/shard_map/all_gather | solution.py:12
  78.2 6.4 %copy-start.5 = (s32[2]{0:T(128)S(1)}, s32[2]{0:T(128)}, u32[]{:S(2)}) copy-start(s32[2]{0:T(128)} %param.11) | copy-start | bytes 28
  78.2 6.5 %copy-start.3 = (f32[2,2,2,128,128]{4,3,1,2,0:T(8,128)S(1)}, f32[2,2,2,128,128]{4,3,1,2,0:T(8,128)}, u32[]{:S(2)}) copy-start(f32[2,2,2,128,128]{4,3,1,2,0:T(8,128)} %get-tuple-element.194) | copy-start | bytes 1572868
  83.8 1.0 copy-start.4
Sparse Core Ops, SparseCore 0:
  78.2 96.4 all-gather.6
  177.9 100.7 all-gather.4
where the time goes:
time: 359 us; the launch traced here: 358 us
  waiting for transfers between devices  240 us (67%)
  matrix products  46.8 us (13%)
  local copies, waits for them, and re-layouts  40.9 us (11%)
  between operations  14.2 us (4%)
  starting transfers between devices  7.29 us (2%)
  other arithmetic  5.63 us (2%)
    all_gather x2, waiting for transfers between devices, entering(): gathered = lax.all_gather(part, axis)  191 us
    all_to_all x1, waiting for transfers between devices, shards(): lax.all_to_all(sections, 'wl', split_axis=1, concat_axis=4, tiled=True)  49.2 us
    dot_general x148, matrix products, matrix_product(): return jnp.matmul(outer_mat, inner_mat, precision=lax.Precision.HIGHEST)  40 us
    squeeze x31, local copies, waits for them, and re-layouts, one(): return combine(state, lax.dynamic_index_in_dim(gathered, source, 0, False))  30.1 us
    all_to_all x1, starting transfers between devices, shards(): lax.all_to_all(sections, 'wl', split_axis=1, concat_axis=4, tiled=True)  7.21 us
  transfers between devices with their start and end apart: 3, of which 3 were waited for; matrix products, arithmetic and copies ran while one was open for 2% of the time, Pallas kernels for 0%

commit v1 on v0

--- a/solution.py
+++ b/solution.py
@@ -52,7 +52,10 @@
 
 
 def shards(sections, launch_mode):
-    regrouped = lax.all_to_all(sections, "wl", split_axis=1, concat_axis=4, tiled=True)
+    regrouped = jnp.concatenate(
+        lax.all_to_all(jnp.stack(jnp.split(sections, lax.axis_size("wl"), axis=1)), "wl", 0, 0),
+        axis=4,
+    )
     forward_mats = regrouped[:, :, 0]
     backward_mats = regrouped[:, :, 1]
     modes = forward_mats.shape[-1]

time: 359 us -> 379 us (1.056)
  local copies, waits for them, and re-layouts: 40.9 us -> 61.3 us
    unnamed x9 -> x21, local copies, waits for them, and re-layouts: 4.63 us -> 23.6 us
where the time goes in v1:
time: 379 us; the launch traced here: 378 us
  waiting for transfers between devices  241 us (64%)
  local copies, waits for them, and re-layouts  61.3 us (16%)
  matrix products  46.3 us (12%)
  between operations  14.3 us (4%)
  starting transfers between devices  7.34 us (2%)
  other arithmetic  5.61 us (1%)
    all_gather x2, waiting for transfers between devices, entering(): gathered = lax.all_gather(part, axis)  191 us
    all_to_all x1, waiting for transfers between devices, shards(): lax.all_to_all(jnp.stack(jnp.split(sections, lax.axis_size('wl'), axis=1)...  49.2 us
    dot_general x148, matrix products, matrix_product(): return jnp.matmul(outer_mat, inner_mat, precision=lax.Precision.HIGHEST)  39.5 us
    squeeze x31, local copies, waits for them, and re-layouts, one(): return combine(state, lax.dynamic_index_in_dim(gathered, source, 0, False))  30.1 us
    unnamed x21, local copies, waits for them, and re-layouts  23.6 us
  transfers between devices with their start and end apart: 3, of which 3 were waited for; matrix products, arithmetic and copies ran while one was open for 2% of the time, Pallas kernels for 0%

profile of v1, /device:TPU:454, one launch (start us, length us, event | category | flops | bytes accessed | tf_op | source)
XLA Modules:
  0.0 377.5 jit_solution(12831210185925235947)
XLA Ops:
  7.2 1.6 bitcast_dynamic-update-slice_fusion.17
  8.7 1.6 bitcast_dynamic-update-slice_fusion.16
  10.3 1.6 bitcast_dynamic-update-slice_fusion.15
  11.9 1.6 bitcast_dynamic-update-slice_fusion.14
  13.4 1.6 bitcast_dynamic-update-slice_fusion.13
  15.0 1.6 bitcast_dynamic-update-slice_fusion.12
  16.6 1.6 bitcast_dynamic-update-slice_fusion.11
  18.1 1.6 bitcast_dynamic-update-slice_fusion.10
  19.7 1.6 bitcast_dynamic-update-slice_fusion.9
  21.3 1.6 bitcast_dynamic-update-slice_fusion.8
  22.8 1.6 bitcast_dynamic-update-slice_fusion.7
  24.4 1.6 bitcast_dynamic-update-slice_fusion.6
  25.9 1.6 bitcast_dynamic-update-slice_fusion.5
  27.5 1.6 bitcast_dynamic-update-slice_fusion.4
  29.1 1.6 bitcast_dynamic-update-slice_fusion.3
  30.6 1.6 bitcast_dynamic-update-slice_fusion.2
  32.2 7.3 %all-to-all-start = ((f32[16,4,2,2,2,8,128]{6,5,4,3,2,1,0:T(8,128)}), f32[16,4,2,2,2,8,128]{6,5,4,3,2,1,0:T(8,128)}, u32[]{:S(2)}, u32[]{:S(2)}) async-start(f32[16,4,2,2,2,8,128]{6,5,4,3,2,1,0:T(8,128)} %bitcast_dynamic-update-slice_fusion.2), calls=%async_computation | async-start | bytes 4194304 | tf_op jit(solution)/shard_map/all_to_all | solution.py:56
  39.5 49.2 %all-to-all-done = f32[16,4,2,2,2,8,128]{6,5,4,3,2,1,0:T(8,128)} async-done(((f32[16,4,2,2,2,8,128]{6,5,4,3,2,1,0:T(8,128)}), f32[16,4,2,2,2,8,128]{6,5,4,3,2,1,0:T(8,128)}, u32[]{:S(2)}, u32[]{:S(2)}) %all-to-all-start) | async-done | bytes 2097184 | tf_op jit(solution)/shard_map/all_to_all | solution.py:56
  88.8 1.8 copy_bitcast_fusion.1
  90.7 0.8 slice_bitcast_fusion.26
  91.5 0.9 broadcast_in_dim.33
  92.3 4.0 %while.52 = (s32[]{:T(128)}, f32[2,2,128,128]{3,2,0,1:T(8,128)S(1)}, f32[2,2,2,128,128]{4,3,1,2,0:T(8,128)}, f32[2,2,2,128,128]{4,3,1,2,0:T(8,128)S(1)}, s32[]{:T(128)}) while((s32[]{:T(128)}, f32[2,2,128,128]{3,2,0,1:T(8,128)S(1)}, f32[2,2,2,128,128]{4,3,1,2,0:T(8,128)}, f32[2,2,2,128,128]{4,3,1,2,0:T(8,128)S(1)}, s32[]{:T(128)}) %tuple.105), condition=%wide.region_5.6_spmd, body=%wide.region_4.5_spmd.sunk | while | flops 201457664 | bytes 7602313 | solution.py:77
  93.5 0.8 copy-done.1
  95.5 0.8 copy-done.1
  98.3 5.6 %while.50 = (s32[]{:T(128)}, f32[2,2,128,128]{3,2,0,1:T(8,128)S(1)}, f32[3,2,2,128,128]{4,3,1,2,0:T(8,128)}, f32[3,2,2,128,128]{4,3,1,2,0:T(8,128)S(1)}, s32[]{:T(128)}) while((s32[]{:T(128)}, f32[2,2,128,128]{3,2,0,1:T(8,128)S(1)}, f32[3,2,2,128,128]{4,3,1,2,0:T(8,128)}, f32[3,2,2,128,128]{4,3,1,2,0:T(8,128)S(1)}, s32[]{:T(128)}) %tuple.99), condition=%wide.region_1.2_spmd, body=%wide.region_0.1_spmd.sunk | while | flops 201457664 | bytes 3145805 | solution.py:71
  99.4 0.7 bitcast_dynamic-update-slice_fusion.20
  101.3 0.7 bitcast_dynamic-update-slice_fusion.20
  103.1 0.7 bitcast_dynamic-update-slice_fusion.20
  103.9 0.7 copy.11
  104.9 1.2 fusion.51
  106.1 88.7 %all-gather.7.cloned.1.call-done = f32[64,2,128,128]{3,2,0,1:T(8,128)} async-done(((f32[2,2,128,128]{3,2,0,1:T(8,128)}), f32[64,2,128,128]{3,2,0,1:T(8,128)}) %all-gather.7.cloned.1.call-update) | async-done | bytes 8388624 | tf_op jit(solution)/shard_map/all_gather | solution.py:12
  196.1 102.6 %all-gather.5.cloned.1.call-done = f32[64,2,128,128]{3,2,1,0:T(8,128)} async-done(((f32[2,2,128,128]{3,2,1,0:T(8,128)}), f32[64,2,128,128]{3,2,1,0:T(8,128)}) %all-gather.5.cloned.1.call-update) | async-done | bytes 8388624 | tf_op jit(solution)/shard_map/all_gather | solution.py:12
  298.7 65.7 %while.51 = (s32[]{:T(128)}, f32[2,2,128,128]{3,2,0,1:T(8,128)S(1)}, s32[]{:T(128)}, f32[32,2,2,128,128]{4,3,2,1,0:T(8,128)}, s32[]{:T(128)}, /*index=5*/s32[]{:T(128)}, s32[]{:T(128)}) while((s32[]{:T(128)}, f32[2,2,128,128]{3,2,0,1:T(8,128)S(1)}, s32[]{:T(128)}, f32[32,2,2,128,128]{4,3,2,1,0:T(8,128)}, s32[]{:T(128)}, /*index=5*/s32[]{:T(128)}, ...), condition=%wide.region_3.4_spmd, body=%wide.region_2.3_spmd.sunk | while | flops 201457664 | bytes 2883707 | solution.py:19
  298.7 1.0 copy_bitcast_fusion.3
  300.8 1.0 copy_bitcast_fusion.3
  303.0 1.0 copy_bitcast_fusion.3
  305.1 1.0 copy_bitcast_fusion.3
  307.2 1.0 copy_bitcast_fusion.3
  309.3 1.0 copy_bitcast_fusion.3
  311.4 1.0 copy_bitcast_fusion.3
  313.6 1.0 copy_bitcast_fusion.3
  315.7 1.0 copy_bitcast_fusion.3
  317.8 1.0 copy_bitcast_fusion.3
  319.9 1.0 copy_bitcast_fusion.3
  322.0 1.0 copy_bitcast_fusion.3
  324.2 1.0 copy_bitcast_fusion.3
  326.3 1.0 copy_bitcast_fusion.3
  328.4 1.0 copy_bitcast_fusion.3
  330.5 1.0 copy_bitcast_fusion.3
  332.6 1.0 copy_bitcast_fusion.3
  334.8 1.0 copy_bitcast_fusion.3
  336.9 1.0 copy_bitcast_fusion.3
  339.0 1.0 copy_bitcast_fusion.3
  341.1 1.0 copy_bitcast_fusion.3
  343.2 1.0 copy_bitcast_fusion.3
  345.4 1.0 copy_bitcast_fusion.3
  347.5 1.0 copy_bitcast_fusion.3
  349.6 1.0 copy_bitcast_fusion.3
  351.7 1.0 copy_bitcast_fusion.3
  353.9 1.0 copy_bitcast_fusion.3
  356.0 1.0 copy_bitcast_fusion.3
  358.1 1.0 copy_bitcast_fusion.3
  360.2 1.0 copy_bitcast_fusion.3
  362.3 1.0 copy_bitcast_fusion.3
  (242 shorter events, 49.0 us)
Async XLA Ops:
  32.2 56.6 %all-to-all-start = ((f32[16,4,2,2,2,8,128]{6,5,4,3,2,1,0:T(8,128)}), f32[16,4,2,2,2,8,128]{6,5,4,3,2,1,0:T(8,128)}, u32[]{:S(2)}, u32[]{:S(2)}) async-start(f32[16,4,2,2,2,8,128]{6,5,4,3,2,1,0:T(8,128)} %bitcast_dynamic-update-slice_fusion.2), calls=%async_computation | async-start | bytes 4194304 | tf_op jit(solution)/shard_map/all_to_all | solution.py:56
  39.5 155.3 %all-gather.7.cloned.1.call-start = ((), (), s32[]{:S(2)}) async-start(), calls=%async_computation.2 | async-start | bytes 8650752 | tf_op jit(solution)/shard_map/all_gather | solution.py:12
  92.3 1.1 copy-start
  93.5 0.8 copy-start.1
  94.3 1.1 copy-start
  95.5 0.8 copy-start.1
  98.1 200.6 %all-gather.5.cloned.1.call-start = ((), (), s32[]{:S(2)}) async-start(), calls=%async_computation.1 | async-start | bytes 8650752 | tf_op jit(solution)/shard_map/all_gather | solution.py:12
  98.2 6.4 %copy-start.4 = (s32[2]{0:T(128)S(1)}, s32[2]{0:T(128)}, u32[]{:S(2)}) copy-start(s32[2]{0:T(128)} %param.11) | copy-start | bytes 28
  98.2 6.5 %copy-start.2 = (f32[2,2,2,128,128]{4,3,1,2,0:T(8,128)S(1)}, f32[2,2,2,128,128]{4,3,1,2,0:T(8,128)}, u32[]{:S(2)}) copy-start(f32[2,2,2,128,128]{4,3,1,2,0:T(8,128)} %get-tuple-element.194) | copy-start | bytes 1572868
  103.9 1.0 copy-start.3
Sparse Core Ops, SparseCore 0:
  98.2 96.4 all-gather.6
  197.9 100.6 all-gather.4
